TPU v7x, 256 devices: a whole 4x4x8 slice. The times are simulated.
256 devices in a mesh: row: 8 (over z), col: 32 (over x, y, core).
Axes of the slice: x: 4, y: 4, z: 8, core: 2. Of those that a mesh axis runs over, the one named last changes fastest.
Arguments:
- tile_data: bfloat16 [8, 32, 32, 256, 256], P('row', 'col'), may hold values from -0.125 to 0.125
- tile_row_block: int32 [8, 32, 32], P('row', 'col'), may hold values from 0 to 63
- tile_column_block: int32 [8, 32, 32], P('row', 'col'), may hold values from 0 to 63
- tile_count: int32 [8, 32], P('row', 'col'), may hold values from 1 to 32, as said below
- saved_primal: float32 [3, 524288], P(None, 'col'), may hold values from 0 to 1
- saved_dual: float32 [3, 131072], P(None, 'row'), may hold values from 0 to 1
- primal_mask: int32 [3, 524288], P(None, 'col'), may hold values 0 or 1
- dual_mask: int32 [3, 131072], P(None, 'row'), may hold values 0 or 1
- cost_vector: float32 [524288], P('col'), may hold values from -6 to 6
- demand: float32 [131072], P('row'), may hold values from -6 to 6
- upper_bound: float32 [524288], P('col'), may hold values from 0.5 to 1.5
- step_sizes: float32 [2], replicated, may hold values from 0.2 to 0.4
- primal_cotangent: float32 [524288], P('col'), may hold values from -6 to 6
- dual_cotangent: float32 [131072], P('row'), may hold values from -6 to 6
Outputs:
- primal_adjoint: float32 [524288], P('col')
- dual_adjoint: float32 [131072], P(('row', 'col'))
- step_gradients: float32 [2], replicated
Inputs may be any that keep to these rules, and one draw needn't show every extreme that they name: `tile_count`: block positions may repeat, and tiles at one position add; slots at and beyond a device's count are ignored. In every index of row some device has 32 live slots.
All inputs are finite; a program needn't handle non-finite values. No bound on the sum of `primal_mask` or of `dual_mask` on one device may be relied on, other than what follows from the above.
Results may differ from a plain program's by a relative error of at most 0.00071.
Values may be sent and summed in bfloat16 or wider, within the bound.
A program may use at most 64 MiB of HBM per device.

v0:
```python
import math

import jax
import jax.numpy as jnp
from jax import lax
from jax.sharding import PartitionSpec as P


def block_terms(tile_part, in_part, out_part, live_part, vectors, out_blocks, transpose):
    tile_width = tile_part.shape[-1]
    blocks = vectors.reshape(vectors.shape[0], -1, tile_width)
    picked = jnp.take(blocks, in_part, axis=1)
    einsum_form = "sij,bsi->bsj" if transpose else "sij,bsj->bsi"
    products = jnp.einsum(einsum_form, tile_part, picked, preferred_element_type=jnp.float32)
    products = products * live_part[None, :, None]
    selector = (out_part[:, None] == jnp.arange(out_blocks, dtype=jnp.int32)[None, :]).astype(
        jnp.float32
    )
    summed = jnp.einsum("sn,bsi->bni", selector, products, precision=lax.Precision.HIGHEST)
    return summed.reshape(vectors.shape[0], out_blocks * tile_width)


def tile_apply(tile_stack, in_index, out_index, live_count, vectors, out_blocks, transpose):
    slot_count = tile_stack.shape[0]
    live_slots = (jnp.arange(slot_count, dtype=jnp.int32) < live_count).astype(jnp.float32)
    return block_terms(tile_stack, in_index, out_index, live_slots, vectors, out_blocks, transpose)


def local(
    tile_data,
    tile_row_block,
    tile_column_block,
    tile_count,
    saved_primal,
    saved_dual,
    primal_mask,
    dual_mask,
    cost_vector,
    demand,
    upper_bound,
    step_sizes,
    primal_cotangent,
    dual_cotangent,
):
    slot_count = tile_data.shape[2]
    tile_width = tile_data.shape[-1]
    tile_stack = tile_data.reshape(slot_count, tile_width, tile_width)
    row_blocks = tile_row_block.reshape(slot_count)
    column_blocks = tile_column_block.reshape(slot_count)
    live_count = tile_count.reshape(())
    iterations = saved_primal.shape[0]
    row_length = saved_dual.shape[1]
    column_length = saved_primal.shape[1]
    share_rows = row_length // lax.axis_size("col")
    share_start = lax.axis_index("col") * share_rows
    column_part = column_length // lax.axis_size("row")
    column_start = lax.axis_index("row") * column_part
    tau = step_sizes[0]
    sigma = step_sizes[1]

    def forward(vectors):
        return tile_apply(
            tile_stack,
            column_blocks,
            row_blocks,
            live_count,
            vectors,
            row_length // tile_width,
            False,
        )

    def backward(vectors):
        return tile_apply(
            tile_stack,
            row_blocks,
            column_blocks,
            live_count,
            vectors,
            column_length // tile_width,
            True,
        )

    def row_share(array):
        return lax.dynamic_slice_in_dim(array, share_start, share_rows, array.ndim - 1)

    def column_share(array):
        return lax.dynamic_slice_in_dim(array, column_start, column_part, array.ndim - 1)

    dual_partial = backward(saved_dual.astype(jnp.bfloat16))
    reduced = cost_vector[None, :] - lax.psum(dual_partial, "row")
    half = jnp.clip(saved_primal - tau * reduced, 0.0, upper_bound[None, :])
    extrapolated = (2.0 * half - saved_primal).astype(jnp.bfloat16)
    masks_x = primal_mask.astype(jnp.float32)
    adjoint_x = primal_cotangent
    partial_value = forward(extrapolated)
    residual_share = row_share(demand[None, :] - lax.psum(partial_value, "col"))
    adjoint_y = dual_cotangent
    masks_y = dual_mask.astype(jnp.float32)
    anchor_x = jnp.zeros_like(adjoint_x)
    anchor_y = jnp.zeros_like(adjoint_y)
    tau_sum = jnp.zeros((), jnp.float32)
    sigma_sum = jnp.zeros((), jnp.float32)
    for step in reversed(range(iterations)):
        weight = (step + 1.0) / (step + 2.0)
        anchor_x = anchor_x + (1.0 - weight) * adjoint_x
        anchor_y = anchor_y + (1.0 - weight) * adjoint_y
        dual_term = masks_y[step] * weight * adjoint_y
        sigma_local = jnp.sum(row_share(dual_term) * residual_share[step])
        spread = dual_term.astype(jnp.bfloat16)
        back_partial = backward(spread[None, :])
        back = lax.psum(back_partial, "row")[0]
        primal_term = masks_x[step] * (weight * adjoint_x - 2.0 * sigma * back)
        tau_local = jnp.sum(-column_share(primal_term) * column_share(reduced[step]))
        primal_input = primal_term.astype(jnp.bfloat16)
        adjoint_x = primal_term + sigma * back
        image = forward(primal_input[None, :])
        image_rows = lax.psum(image, "col")[0]
        adjoint_y = dual_term + tau * image_rows
        tau_total, sigma_total = lax.psum((tau_local, sigma_local), ("row", "col"))
        tau_sum = tau_sum + tau_total
        sigma_sum = sigma_sum + sigma_total
    primal_adjoint = adjoint_x + anchor_x
    dual_adjoint = row_share(adjoint_y + anchor_y)
    total_columns = column_length * lax.axis_size("col")
    total_rows = row_length * lax.axis_size("row")
    gradients = jnp.stack([tau_sum / math.sqrt(total_columns), sigma_sum / math.sqrt(total_rows)])
    return (primal_adjoint, dual_adjoint, gradients)


def solution(mesh):
    placed = (
        P("row", "col", None, None, None),
        P("row", "col", None),
        P("row", "col", None),
        P("row", "col"),
        P(None, "col"),
        P(None, "row"),
        P(None, "col"),
        P(None, "row"),
        P("col"),
        P("row"),
        P("col"),
        P(),
        P("col"),
        P("row"),
    )
    return jax.shard_map(
        local,
        mesh=mesh,
        in_specs=placed,
        out_specs=(P("col"), P(("row", "col")), P()),
        check_vma=False,
    )
```

profile of v0, /device:TPU:1, one launch (start us, length us, event | category | flops | bytes accessed | tf_op | source)
XLA Modules:
  0.0 686.6 jit_solution(12237295428847181642)
XLA Ops:
  7.3 0.7 compare_select_fusion
  8.0 0.7 compare_and_fusion
  8.7 1.0 convert_element_type.25
  9.9 0.9 fusion.74
  11.4 0.6 gather_fusion
  12.1 2.8 fusion.14
  15.3 0.7 copy.31
  17.5 68.9 %all-reduce.10.cloned.1.call-done = f32[1,16384]{1,0:T(1,128)} async-done(((f32[1,16384]{1,0:T(1,128)}), f32[1,16384]{1,0:T(1,128)}) %all-reduce.10.cloned.1.call-update) | async-done | bytes 65552 | tf_op jit(solution)/shard_map/psum | solution.py:111
  86.4 1.6 broadcast_multiply_fusion.5
  88.0 0.6 gather_fusion.1
  88.7 3.4 fusion.12
  92.4 0.7 copy.32
  93.3 0.6 gather_fusion.6
  93.9 108.8 %all-reduce.12.cloned.1.call-done = f32[1,16384]{1,0:T(1,128)} async-done(((f32[1,16384]{1,0:T(1,128)}), f32[1,16384]{1,0:T(1,128)}) %all-reduce.12.cloned.1.call-update) | async-done | bytes 65552 | tf_op jit(solution)/shard_map/psum | solution.py:117
  202.7 1.5 broadcast_multiply_fusion.2
  204.2 0.6 gather_fusion.2
  204.9 2.8 fusion.10
  208.1 0.7 copy.33
  208.9 2.9 fusion.2
  211.7 62.4 %all-reduce.14.cloned.1.call-done = f32[1,16384]{1,0:T(1,128)} async-done(((f32[1,16384]{1,0:T(1,128)}), f32[1,16384]{1,0:T(1,128)}) %all-reduce.14.cloned.1.call-update) | async-done | bytes 65552 | tf_op jit(solution)/shard_map/psum | solution.py:111
  274.1 1.6 broadcast_multiply_fusion.4
  275.7 0.6 gather_fusion.3
  276.4 3.4 fusion.8
  280.1 0.7 copy.34
  281.2 0.8 copy.37
  282.1 108.3 %all-reduce.16.cloned.1.call-done = f32[1,16384]{1,0:T(1,128)} async-done(((f32[1,16384]{1,0:T(1,128)}), f32[1,16384]{1,0:T(1,128)}) %all-reduce.16.cloned.1.call-update) | async-done | bytes 65552 | tf_op jit(solution)/shard_map/psum | solution.py:117
  390.4 1.5 broadcast_multiply_fusion.1
  391.9 0.6 gather_fusion.4
  392.7 2.8 fusion.6
  395.8 0.7 copy.35
  396.6 0.8 dynamic-slice.3
  397.3 66.3 %all-reduce.20.cloned.1.call-done = (f32[1,16384]{1,0:T(1,128)}, f32[3,16384]{1,0:T(4,128)}) async-done(((f32[1,16384]{1,0:T(1,128)}, f32[3,16384]{1,0:T(4,128)}), (f32[1,16384]{1,0:T(1,128)}, f32[3,16384]{1,0:T(4,128)})) %all-reduce.20.cloned.1.call-update) | async-done | bytes 262160 | tf_op jit(solution)/shard_map/psum | solution.py:111
  463.7 1.8 subtract_convert_fusion
  465.6 1.6 broadcast_multiply_fusion.3
  467.8 3.4 fusion
  471.6 0.8 copy.38
  472.4 0.7 multiply_reduce_fusion.1
  473.1 0.6 gather_fusion.5
  473.8 3.4 fusion.4
  477.5 0.7 copy.36
  481.4 112.0 %all-reduce.18.cloned.1.call-done = (f32[1,16384]{1,0:T(1,128)}, f32[3,16384]{1,0:T(4,128)}) async-done(((f32[1,16384]{1,0:T(1,128)}, f32[3,16384]{1,0:T(4,128)}), (f32[1,16384]{1,0:T(1,128)}, f32[3,16384]{1,0:T(4,128)})) %all-reduce.18.cloned.1.call-update) | async-done | bytes 262160 | tf_op jit(solution)/shard_map/psum | solution.py:117
  593.4 0.7 dynamic-slice_subtract_fusion
  594.1 0.7 multiply_reduce_fusion.4
  594.8 0.7 multiply_reduce_fusion.5
  595.5 1.5 broadcast_multiply_fusion
  598.3 1.9 multiply_reduce_fusion.3
  600.9 0.7 add_add_fusion
  601.5 76.4 %all-reduce = (f32[]{:T(128)}, f32[]{:T(128)}) all-reduce(f32[]{:T(128)S(6)} %add.120, f32[]{:T(128)S(6)} %add.118), channel_id=1, replica_groups=mesh['row'=8,'col'=32] {'row','col'}, use_global_device_ids=true, to_apply=%region_15.18 | all-reduce | flops 2 | bytes 16 | tf_op jit(solution)/shard_map/psum | solution.py:119
  (72 shorter events, 7.2 us)
Async XLA Ops:
  7.2 7.8 %copy-start.6 = (s32[1,1,32]{2,1,0:T(1,128)S(1)}, s32[1,1,32]{2,1,0:T(1,128)}, u32[]{:S(2)}) copy-start(s32[1,1,32]{2,1,0:T(1,128)} %param.20) | copy-start | bytes 388
  7.2 8.9 %copy-start.8 = (f32[2]{0:T(128)S(1)}, f32[2]{0:T(128)}, u32[]{:S(2)}) copy-start(f32[2]{0:T(128)} %param.29) | copy-start | bytes 28
  7.2 9.4 %copy-start.1 = (s32[3,16384]{1,0:T(4,128)S(1)}, s32[3,16384]{1,0:T(4,128)}, u32[]{:S(2)}) copy-start(s32[3,16384]{1,0:T(4,128)} %param.24) | copy-start | bytes 589828
  7.2 80.8 %copy-start.3 = (f32[16384]{0:T(1024)S(1)}, f32[16384]{0:T(1024)}, u32[]{:S(2)}) copy-start(f32[16384]{0:T(1024)} %param.30) | copy-start | bytes 196612
  7.2 79.2 %all-reduce.10.cloned.1.call-start = ((), (), s32[]{:S(2)}) async-start(), calls=%async_computation | async-start | bytes 131072 | tf_op jit(solution)/shard_map/psum | solution.py:111
  14.9 77.1 %copy-start.7 = (s32[1,1,32]{2,1,0:T(1,128)S(1)}, s32[1,1,32]{2,1,0:T(1,128)}, u32[]{:S(2)}) copy-start(s32[1,1,32]{2,1,0:T(1,128)} %param.19) | copy-start | bytes 388
  14.9 78.2 %copy-start = (f32[3,16384]{1,0:T(4,128)S(1)}, f32[3,16384]{1,0:T(4,128)}, u32[]{:S(2)}) copy-start(f32[3,16384]{1,0:T(4,128)} %param.23) | copy-start | bytes 589828
  16.0 186.7 %all-reduce.12.cloned.1.call-start = ((), (), s32[]{:S(2)}) async-start(), calls=%async_computation.1 | async-start | bytes 131072 | tf_op jit(solution)/shard_map/psum | solution.py:117
  93.1 181.0 %all-reduce.14.cloned.1.call-start = ((), (), s32[]{:S(2)}) async-start(), calls=%async_computation.2 | async-start | bytes 131072 | tf_op jit(solution)/shard_map/psum | solution.py:111
  208.8 181.6 %all-reduce.16.cloned.1.call-start = ((), (), s32[]{:S(2)}) async-start(), calls=%async_computation.3 | async-start | bytes 131072 | tf_op jit(solution)/shard_map/psum | solution.py:117
  279.8 183.9 %copy-start.2 = (f32[3,16384]{1,0:T(4,128)S(1)}, f32[3,16384]{1,0:T(4,128)}, u32[]{:S(2)}) copy-start(f32[3,16384]{1,0:T(4,128)} %param.22) | copy-start | bytes 589828
  279.8 183.9 %copy-start.4 = (f32[16384]{0:T(1024)S(1)}, f32[16384]{0:T(1024)}, u32[]{:S(2)}) copy-start(f32[16384]{0:T(1024)} %param.28) | copy-start | bytes 196612
  279.8 183.9 %copy-start.5 = (f32[16384]{0:T(1024)S(1)}, f32[16384]{0:T(1024)}, u32[]{:S(2)}) copy-start(f32[16384]{0:T(1024)} %param.26) | copy-start | bytes 196612
  280.8 182.9 %all-reduce.20.cloned.1.call-start = ((), (), s32[]{:S(2)}) async-start(), calls=%async_computation.5 | async-start | bytes 655360 | tf_op jit(solution)/shard_map/psum | solution.py:111
  396.5 196.9 %all-reduce.18.cloned.1.call-start = ((), (), s32[]{:S(2)}) async-start(), calls=%async_computation.4 | async-start | bytes 655360 | tf_op jit(solution)/shard_map/psum | solution.py:117
Sparse Core Ops, SparseCore 0:
  16.1 70.2 all-reduce.9
  93.3 109.3 all-reduce.11
  208.9 65.1 all-reduce.13
  280.9 109.3 all-reduce.15
  396.6 66.9 all-reduce.19
  478.4 114.9 all-reduce.17
where the time goes:
time: 688 us; the launch traced here: 687 us
  waiting for transfers between devices  527 us (77%)
  blocking collectives  76.4 us (11%)
  matrix products  27.4 us (4%)
  other arithmetic  22.2 us (3%)
  between operations  20.9 us (3%)
  local copies, waits for them, and re-layouts  12.7 us (2%)
    psum x3, waiting for transfers between devices, local(): image_rows = lax.psum(image, 'col')[0]  329 us
    psum x3, waiting for transfers between devices, local(): back = lax.psum(back_partial, 'row')[0]  198 us
    psum x1, blocking collectives, local(): tau_total, sigma_total = lax.psum((tau_local, sigma_local), ('row', 'col'))  76.4 us
    dot_general x8, matrix products, block_terms(): jnp.einsum(einsum_form, tile_part, picked, preferred_element_type=jnp.flo...  24.8 us
  transfers between devices with their start and end apart: 6, of which 6 were waited for; matrix products, arithmetic and copies ran while one was open for 1% of the time, Pallas kernels for 0%

commit v1 on v0

v1 whole, which is shorter than its diff:
```python
import functools
import math

import jax
import jax.numpy as jnp
from jax import lax
from jax.experimental import pallas as pl
from jax.experimental.pallas import tpu as pltpu
from jax.sharding import PartitionSpec as P

F32 = jnp.float32
BF16 = jnp.bfloat16
LANES = 128
NN = (((1,), (0,)), ((), ()))
NT = (((1,), (1,)), ((), ()))


def ring_offsets(n):
    return sorted(range(1, n), key=lambda r: -min(r, n - r))


def kernel(
    dims,
    tiles_hbm,
    rb_hbm,
    cb_hbm,
    count_hbm,
    primal_hbm,
    dual_hbm,
    pmask_hbm,
    dmask_hbm,
    cost_hbm,
    demand_hbm,
    upper_hbm,
    steps_hbm,
    pcot_hbm,
    dcot_hbm,
    padj_hbm,
    dadj_hbm,
    grad_hbm,
    tiles,
    rb_s,
    cb_s,
    count_s,
    steps_s,
    primal_in,
    dual_in,
    pmask_in,
    dmask_in,
    cost,
    demand,
    upper,
    pcot,
    dcot,
    primal,
    pmask,
    dmask,
    lhs,
    hi_rows,
    lo_rows,
    p_rows,
    z_send,
    z_recv,
    z3_send,
    z3_recv,
    hilo,
    p_all,
    x_all,
    c_lin,
    c_send,
    c_recv,
    d_all,
    out_all,
    dadj,
    sz_all,
    sc_all,
    grad,
    in_sem,
    send_sem,
    recv_sem,
):
    n_row, n_col, iters, slots = dims
    me_r = lax.axis_index("row")
    me_c = lax.axis_index("col")
    blocks = 64
    width = tiles.shape[-1]

    def fetch(i, src, dst):
        copy = pltpu.make_async_copy(src, dst, in_sem.at[i])
        copy.start()
        return copy

    z_lanes = primal_in.shape[1]
    small = [
        fetch(0, rb_hbm, rb_s),
        fetch(1, cb_hbm, cb_s),
        fetch(2, count_hbm, count_s),
        fetch(3, steps_hbm, steps_s),
        fetch(4, dmask_hbm, dmask_in),
        fetch(5, dcot_hbm, dcot),
    ]
    tile_copy = fetch(6, tiles_hbm, tiles)
    z_at = pl.ds(pl.multiple_of(me_r * z_lanes, LANES), z_lanes)
    rest = [
        fetch(7, dual_hbm, dual_in),
        fetch(8, primal_hbm.at[:, z_at], primal_in),
        fetch(9, pmask_hbm.at[:, z_at], pmask_in),
        fetch(10, cost_hbm.at[me_r], cost),
        fetch(11, upper_hbm.at[me_r], upper),
        fetch(12, pcot_hbm.at[me_r], pcot),
        fetch(13, demand_hbm.at[me_c], demand),
    ]

    z_peers = [(r, lax.rem(me_r + r, n_row)) for r in ring_offsets(n_row)]
    c_peers = [(r, lax.rem(me_c + r, n_col)) for r in range(1, n_col)]
    barrier = pltpu.get_barrier_semaphore()
    for _, r in z_peers:
        pl.semaphore_signal(barrier, inc=1, device_id={"row": r})
    for _, c in c_peers:
        pl.semaphore_signal(barrier, inc=1, device_id={"col": c})

    def send(sem, src, dst, peer):
        pltpu.make_async_remote_copy(
            src_ref=src,
            dst_ref=dst,
            send_sem=send_sem.at[sem],
            recv_sem=recv_sem.at[sem],
            device_id=peer,
            device_id_type=pl.DeviceIdType.MESH,
        ).start()

    def arrive(sem, ref):
        pltpu.make_async_copy(ref, ref, recv_sem.at[sem]).wait()

    def left(sem, ref):
        pltpu.make_async_copy(ref, ref, send_sem.at[sem]).wait()

    iota = lax.broadcasted_iota(jnp.int32, (blocks, LANES), 0)

    def spread(s, index_ref, halves):
        keep = iota == index_ref[0, s] + blocks * jnp.maximum(s + 1 - count_s[0, 0], 0)
        return [
            jnp.where(keep, jnp.broadcast_to(h, (blocks, LANES)), 0.0).astype(BF16) for h in halves
        ]

    def apply_transpose(vectors, pick):
        for s in range(slots):
            for v, halves in enumerate(pick(s)):
                for h, value in enumerate(spread(s, cb_s, halves)):
                    lhs[
                        v * blocks : (v + 1) * blocks,
                        s * width + h * LANES : s * width + (h + 1) * LANES,
                    ] = value
        return lax.dot_general(
            lhs[: vectors * blocks, :],
            tiles[...].reshape(slots * width, width),
            NN,
            preferred_element_type=F32,
        )

    def apply_forward():
        acc = jnp.zeros((blocks, width), F32)
        for s in range(slots):
            c = cb_s[0, s]
            b = lax.div(c, 8)
            i = 2 * lax.rem(c, 8)
            halves = [p_rows[b, pl.ds(i, 1), :], p_rows[b, pl.ds(i + 1, 1), :]]
            row = jnp.concatenate(spread(s, rb_s, halves), axis=1)
            acc = acc + lax.dot_general(row, tiles[s], NT, preferred_element_type=F32)
        return acc

    def store_z(dst, value):
        for j in range(n_row):
            for h in range(2):
                dst[j, pl.ds(h, 8, stride=2), :] = value[
                    8 * j : 8 * j + 8, h * LANES : (h + 1) * LANES
                ]

    for copy in small:
        copy.wait()
    tau = steps_s[0, 0]
    sigma = steps_s[0, 1]
    weights = [(k + 1.0) / (k + 2.0) for k in range(iters)]
    last = iters - 1

    def pick_start(s):
        r = rb_s[0, s]
        a = lax.div(r, 2)
        b = 2 * lax.rem(r, 2)
        his, los = [], []
        for h in range(2):
            mask = dmask_in[pl.ds(last, 1), pl.ds((2 * r + h) * LANES, LANES)]
            d = mask.astype(F32) * weights[last] * dcot[a, pl.ds(b + h, 1), :]
            hi = d.astype(BF16).astype(F32)
            his.append(hi)
            los.append(d - hi)
        return [his, los]

    def pick_d(s):
        r = rb_s[0, s]
        a = lax.div(r, 2)
        b = 2 * lax.rem(r, 2)
        return [
            [ref[a, pl.ds(b, 1), :], ref[a, pl.ds(b + 1, 1), :]] for ref in (hi_rows, lo_rows)
        ]

    def pick_dual(s):
        r = rb_s[0, s]
        return [
            [dual_in[pl.ds(k, 1), pl.ds((2 * r + h) * LANES, LANES)] for h in range(2)]
            for k in range(iters)
        ]

    def phase(k, which):
        return 4 * k + which

    Z3, XG, OUT, SZ, SC = (4 * iters + i for i in range(5))

    tile_copy.wait()

    tau_local = jnp.zeros((), F32)
    sigma_local = jnp.zeros((), F32)
    anchor_x = anchor_y = None
    ax = ay = d = None

    for k in reversed(range(iters)):
        weight = weights[k]
        if k == last:
            both = apply_transpose(2, pick_start)
        else:
            got = d_all[k]
            hi = got.astype(BF16).astype(F32)
            hi_rows[...] = hi
            lo_rows[...] = got - hi
            both = apply_transpose(2, pick_d)
        store_z(z_send.at[k], both[:blocks])
        if k == last:
            pl.semaphore_wait(barrier, len(z_peers) + len(c_peers))
        for r, peer in z_peers:
            send(phase(k, 0), z_send.at[k, peer], z_recv.at[k, r - 1], {"row": peer})
        store_z(hilo.at[k], both[:blocks] + both[blocks:])
        if k == last:
            for copy in rest:
                copy.wait()
            duals = apply_transpose(iters, pick_dual)
            for i in range(iters):
                for j in range(n_row):
                    for h in range(2):
                        z3_send[j, i, pl.ds(h, 8, stride=2), :] = duals[
                            i * blocks + 8 * j : i * blocks + 8 * j + 8,
                            h * LANES : (h + 1) * LANES,
                        ]
            for i in range(iters):
                for q in range(16):
                    cut = slice(q * LANES, (q + 1) * LANES)
                    primal[i, q : q + 1, :] = primal_in[i : i + 1, cut]
                    pmask[i, q : q + 1, :] = pmask_in[i : i + 1, cut].astype(F32)
                for q in range(4):
                    at = pl.multiple_of(me_c * (4 * LANES) + q * LANES, LANES)
                    dmask[i, q : q + 1, :] = dmask_in[i : i + 1, pl.ds(at, LANES)].astype(F32)
            ax = pcot[...]
            ay = dcot[me_c]
            anchor_x = (1.0 - weight) * ax
            anchor_y = (1.0 - weight) * ay
            d = dmask[k] * weight * ay
        else:
            if k == last - 1:
                arrive(XG, x_all.at[pl.ds(0, n_row - 1)])
                part = hilo[last] * x_all[:, last].astype(F32)
                sigma_local = sigma_local - jnp.sum(part)
            part = hilo[k] * x_all[:, k].astype(F32)
            sigma_local = sigma_local - jnp.sum(part)
        sigma_local = sigma_local + jnp.sum(d * demand[...])
        arrive(phase(k, 0), z_recv.at[k])
        back = z_send[k, me_r]
        for r in range(n_row - 1):
            back = back + z_recv[k, r]
        if k != last:
            anchor_x = anchor_x + (1.0 - weight) * ax
        p = pmask[k] * (weight * ax - (2.0 * sigma) * back)
        p_all[k, me_r] = p.astype(BF16)
        for _, peer in z_peers:
            send(phase(k, 1), p_all.at[k, me_r], p_all.at[k, me_r], {"row": peer})
        ax = p + sigma * back
        if k == 0:
            out_all[me_r] = ax + anchor_x
            for _, peer in z_peers:
                send(OUT, out_all.at[me_r], out_all.at[me_r], {"row": peer})
        if k == last:
            p_last = p
        else:
            tau_local = tau_local - jnp.sum(p * primal[k])
        if k == 0:
            lane = lax.broadcasted_iota(jnp.int32, (1, LANES), 1)
            sz_all[me_r] = jnp.where(lane == 0, tau_local, jnp.where(lane == 1, sigma_local, 0.0))
            for _, peer in z_peers:
                send(SZ, sz_all.at[me_r], sz_all.at[me_r], {"row": peer})
        arrive(phase(k, 1), p_all.at[k, pl.ds(0, n_row - 1)])
        if k == last:
            for r, peer in z_peers:
                send(Z3, z3_send.at[peer], z3_recv.at[r - 1], {"row": peer})
        p_rows[...] = p_all[k].astype(F32)
        image = apply_forward()
        c_lin[pl.ds(0, blocks, stride=2), :] = image[:, :LANES]
        c_lin[pl.ds(1, blocks, stride=2), :] = image[:, LANES:]
        c_send[k] = c_lin[...].reshape(n_col, 4, LANES)
        for r, peer in c_peers:
            send(phase(k, 2), c_send.at[k, peer], c_recv.at[k, r - 1], {"col": peer})
        if k == 0:
            arrive(SZ, sz_all.at[pl.ds(0, n_row - 1)])
            total = sz_all[0]
            for r in range(1, n_row):
                total = total + sz_all[r]
            sc_all[me_c] = total
            for _, peer in c_peers:
                send(SC, sc_all.at[me_c], sc_all.at[me_c], {"col": peer})
            arrive(OUT, out_all.at[pl.ds(0, n_row - 1)])
            padj_copy = pltpu.make_async_copy(out_all, padj_hbm, in_sem.at[0])
            padj_copy.start()
        arrive(phase(k, 2), c_recv.at[k])
        rows = c_send[k, me_c]
        for r in range(n_col - 1):
            rows = rows + c_recv[k, r]
        ay = d + tau * rows
        if k > 0:
            weight = weights[k - 1]
            anchor_y = anchor_y + (1.0 - weight) * ay
            d = dmask[k - 1] * weight * ay
            d_all[k - 1, me_c] = d
            for _, peer in c_peers:
                here = d_all.at[k - 1, me_c]
                send(phase(k - 1, 3), here, here, {"col": peer})
            if k == last:
                arrive(Z3, z3_recv)
                for i in range(iters):
                    column = z3_send[me_r, i]
                    for r in range(n_row - 1):
                        column = column + z3_recv[r, i]
                    reduced = cost[...] - column
                    saved = primal[i]
                    half = jnp.minimum(jnp.maximum(saved - tau * reduced, 0.0), upper[...])
                    x_all[me_r, i] = (2.0 * half - saved).astype(BF16)
                    primal[i] = reduced
                for _, peer in z_peers:
                    send(XG, x_all.at[me_r], x_all.at[me_r], {"row": peer})
                tau_local = tau_local - jnp.sum(p_last * primal[last])
            arrive(phase(k - 1, 3), d_all.at[k - 1, pl.ds(0, n_col - 1)])

    dadj[...] = ay + anchor_y
    dadj_copy = pltpu.make_async_copy(dadj, dadj_hbm, in_sem.at[1])
    dadj_copy.start()
    arrive(SC, sc_all.at[pl.ds(0, n_col - 1)])
    total = sc_all[0]
    for c in range(1, n_col):
        total = total + sc_all[c]
    lane = lax.broadcasted_iota(jnp.int32, (1, LANES), 1)
    columns = float(n_col * blocks * width)
    lines = float(n_row * blocks * width)
    grad[...] = total * jnp.where(lane == 0, 1.0 / math.sqrt(columns), 1.0 / math.sqrt(lines))
    grad_copy = pltpu.make_async_copy(grad, grad_hbm, in_sem.at[2])
    grad_copy.start()

    for k in range(iters):
        left(phase(k, 0), z_recv.at[k])
        left(phase(k, 1), p_all.at[k, pl.ds(0, n_row - 1)])
        left(phase(k, 2), c_recv.at[k])
        if k < last:
            left(phase(k, 3), d_all.at[k, pl.ds(0, n_col - 1)])
    left(Z3, z3_recv)
    left(XG, x_all.at[pl.ds(0, n_row - 1)])
    left(OUT, out_all.at[pl.ds(0, n_row - 1)])
    left(SZ, sz_all.at[pl.ds(0, n_row - 1)])
    left(SC, sc_all.at[pl.ds(0, n_col - 1)])
    padj_copy.wait()
    dadj_copy.wait()
    grad_copy.wait()


def local(
    tile_data,
    tile_row_block,
    tile_column_block,
    tile_count,
    saved_primal,
    saved_dual,
    primal_mask,
    dual_mask,
    cost_vector,
    demand,
    upper_bound,
    step_sizes,
    primal_cotangent,
    dual_cotangent,
):
    n_row = lax.axis_size("row")
    n_col = lax.axis_size("col")
    slots, width = tile_data.shape[2], tile_data.shape[-1]
    iters = saved_primal.shape[0]
    rows = saved_dual.shape[1]
    columns = saved_primal.shape[1]
    z_shape = (n_row, columns // n_row // LANES, LANES)
    c_shape = (n_col, rows // n_col // LANES, LANES)
    zq, cq = z_shape[1], c_shape[1]
    blocks = rows // width
    any_spec = pl.BlockSpec(memory_space=pl.ANY)
    phases = 4 * iters + 5
    outs = pl.pallas_call(
        functools.partial(kernel, (n_row, n_col, iters, slots)),
        out_shape=(
            jax.ShapeDtypeStruct(z_shape, F32),
            jax.ShapeDtypeStruct(c_shape[1:], F32),
            jax.ShapeDtypeStruct((1, LANES), F32),
        ),
        in_specs=[any_spec] * 14,
        out_specs=(any_spec,) * 3,
        scratch_shapes=[
            pltpu.VMEM((slots, width, width), BF16),
            pltpu.SMEM((1, slots), jnp.int32),
            pltpu.SMEM((1, slots), jnp.int32),
            pltpu.SMEM((1, 1), jnp.int32),
            pltpu.SMEM((1, 2), F32),
            pltpu.VMEM((iters, columns // n_row), F32),
            pltpu.VMEM((iters, rows), F32),
            pltpu.VMEM((iters, columns // n_row), jnp.int32),
            pltpu.VMEM((iters, rows), jnp.int32),
            pltpu.VMEM(z_shape[1:], F32),
            pltpu.VMEM(c_shape[1:], F32),
            pltpu.VMEM(z_shape[1:], F32),
            pltpu.VMEM(z_shape[1:], F32),
            pltpu.VMEM(c_shape, F32),
            pltpu.VMEM((iters, zq, LANES), F32),
            pltpu.VMEM((iters, zq, LANES), F32),
            pltpu.VMEM((iters, cq, LANES), F32),
            pltpu.VMEM((max(2, iters) * blocks, slots * width), BF16),
            pltpu.VMEM(c_shape, F32),
            pltpu.VMEM(c_shape, F32),
            pltpu.VMEM(z_shape, F32),
            pltpu.VMEM((iters,) + z_shape, F32),
            pltpu.VMEM((iters, n_row - 1, zq, LANES), F32),
            pltpu.VMEM((n_row, iters, zq, LANES), F32),
            pltpu.VMEM((n_row - 1, iters, zq, LANES), F32),
            pltpu.VMEM((iters,) + z_shape, F32),
            pltpu.VMEM((iters,) + z_shape, BF16),
            pltpu.VMEM((n_row, iters, zq, LANES), BF16),
            pltpu.VMEM((rows // LANES, LANES), F32),
            pltpu.VMEM((iters,) + c_shape, F32),
            pltpu.VMEM((iters, n_col - 1, cq, LANES), F32),
            pltpu.VMEM((iters - 1,) + c_shape, F32),
            pltpu.VMEM(z_shape, F32),
            pltpu.VMEM(c_shape[1:], F32),
            pltpu.VMEM((n_row, 1, LANES), F32),
            pltpu.VMEM((n_col, 1, LANES), F32),
            pltpu.VMEM((1, LANES), F32),
            pltpu.SemaphoreType.DMA((14,)),
            pltpu.SemaphoreType.DMA((phases,)),
            pltpu.SemaphoreType.DMA((phases,)),
        ],
        compiler_params=pltpu.CompilerParams(
            collective_id=0, has_side_effects=True, vmem_limit_bytes=40 << 20
        ),
        name="primal_dual_adjoint",
    )(
        tile_data.reshape(slots, width, width),
        tile_row_block.reshape(1, slots),
        tile_column_block.reshape(1, slots),
        tile_count.reshape(1, 1),
        saved_primal,
        saved_dual,
        primal_mask,
        dual_mask,
        cost_vector.reshape(z_shape),
        demand.reshape(c_shape),
        upper_bound.reshape(z_shape),
        step_sizes.reshape(1, 2),
        primal_cotangent.reshape(z_shape),
        dual_cotangent.reshape(c_shape),
    )
    return (outs[0].reshape(columns), outs[1].reshape(rows // n_col), outs[2][0, :2])


def solution(mesh):
    placed = (
        P("row", "col", None, None, None),
        P("row", "col", None),
        P("row", "col", None),
        P("row", "col"),
        P(None, "col"),
        P(None, "row"),
        P(None, "col"),
        P(None, "row"),
        P("col"),
        P("row"),
        P("col"),
        P(),
        P("col"),
        P("row"),
    )
    return jax.shard_map(
        local,
        mesh=mesh,
        in_specs=placed,
        out_specs=(P("col"), P(("row", "col")), P()),
        check_vma=False,
    )
```

time: 688 us -> 88.1 us (0.13)
  waiting for transfers between devices: 527 us -> 0 us
  blocking collectives: 76.4 us -> 0 us
  Pallas kernels: 0 us -> 72.4 us
  matrix products: 27.4 us -> 0 us
  other arithmetic: 22.2 us -> 0 us
  between operations: 20.9 us -> 1.31 us
    psum x6 -> x0, waiting for transfers between devices: 527 us -> none  [the longest x3 329 us: local(): image_rows = lax.psum(image, 'col')[0]]
    psum x1 -> x0, blocking collectives: 76.4 us -> none  [local(): tau_total, sigma_total = lax.psum((tau_local, sigma_local), ('row', 'col'))]
    pallas_call x0 -> x1, Pallas kernels: none -> 72.4 us  [local(): pl.pallas_call(functools.partial(kernel, (n_row, n_col, iters, slots)), o...]
    dot_general x16 -> x0, matrix products: 27.4 us -> none  [the longest x8 24.8 us: block_terms(): jnp.einsum(einsum_form, tile_part, picked, preferred_element_type=jnp.flo...]
    mul x7 -> x0, other arithmetic: 9.44 us -> none  [the longest x3 4.66 us: local(): adjoint_x = primal_term + sigma * back]
    unnamed x26 -> x28, local copies, waits for them, and re-layouts: 5.91 us -> 13.4 us
  transfers between devices with their start and end apart: 6 -> 0, of which waited for: 6 -> 0; matrix products, arithmetic and copies ran while one was open for 1% -> 0% of each run, Pallas kernels for 0% -> 0%
where the time goes in v1:
time: 88.1 us; the launch traced here: 87.5 us
  Pallas kernels  72.4 us (82%)
  local copies, waits for them, and re-layouts  13.9 us (16%)
  between operations  1.31 us (1%)
    pallas_call x1, Pallas kernels, local(): pl.pallas_call(functools.partial(kernel, (n_row, n_col, iters, slots)), o...  72.4 us
    unnamed x28, local copies, waits for them, and re-layouts  13.4 us

profile of v1, /device:TPU:1, one launch (start us, length us, event | category | flops | bytes accessed | tf_op | source)
XLA Modules:
  0.0 87.5 jit_solution(14358351663463034056)
XLA Ops:
  1.3 0.0 copy-start
  1.3 2.2 %copy-done = bf16[1,1,32,256,256]{4,3,2,1,0:T(8,128)(2,1)S(1)} copy-done((bf16[1,1,32,256,256]{4,3,2,1,0:T(8,128)(2,1)S(1)}, bf16[1,1,32,256,256]{4,3,2,1,0:T(8,128)(2,1)}, u32[]{:S(2)}) %copy-start) | copy-done | bytes 4194328
  3.5 0.0 copy-start.1
  3.5 0.9 %copy-done.1 = f32[3,16384]{1,0:T(4,128)S(1)} copy-done((f32[3,16384]{1,0:T(4,128)S(1)}, f32[3,16384]{1,0:T(4,128)}, u32[]{:S(2)}) %copy-start.1) | copy-done | bytes 196632
  4.4 0.0 copy-start.2
  4.4 0.9 %copy-done.2 = f32[3,16384]{1,0:T(4,128)S(1)} copy-done((f32[3,16384]{1,0:T(4,128)S(1)}, f32[3,16384]{1,0:T(4,128)}, u32[]{:S(2)}) %copy-start.2) | copy-done | bytes 196632
  5.4 0.0 copy-start.3
  5.4 0.9 %copy-done.3 = s32[3,16384]{1,0:T(4,128)S(1)} copy-done((s32[3,16384]{1,0:T(4,128)S(1)}, s32[3,16384]{1,0:T(4,128)}, u32[]{:S(2)}) %copy-start.3) | copy-done | bytes 196632
  6.3 0.0 copy-start.4
  6.3 0.9 %copy-done.4 = s32[3,16384]{1,0:T(4,128)S(1)} copy-done((s32[3,16384]{1,0:T(4,128)S(1)}, s32[3,16384]{1,0:T(4,128)}, u32[]{:S(2)}) %copy-start.4) | copy-done | bytes 196632
  7.3 0.0 copy-start.5
  7.3 0.8 copy-done.5
  8.1 0.0 copy-start.6
  8.1 0.8 copy-done.6
  9.0 0.0 copy-start.7
  9.0 0.8 copy-done.7
  9.8 0.0 copy-start.8
  9.8 0.8 copy-done.8
  10.6 0.0 copy-start.9
  10.6 0.8 copy-done.9
  11.5 0.0 copy-start.10
  11.5 0.7 copy-done.10
  12.1 0.0 copy-start.11
  12.1 0.7 copy-done.11
  12.8 0.0 copy-start.12
  12.8 0.7 copy-done.12
  13.4 72.4 %primal_dual_adjoint.1 = (f32[8,16,128]{2,1,0:T(8,128)S(1)}, f32[4,128]{1,0:T(4,128)S(1)}, f32[1,128]{1,0:T(1,128)S(1)}) custom-call(bf16[32,256,256]{2,1,0:T(8,128)(2,1)S(1)} %bitcast.13, s32[1,32]{1,0:T(1,128)S(1)} %bitcast.21, s32[1,32]{1,0:T(1,128)S(1)} %bitcast.22, s32[1,1]{1,0:T(1,128)S(6)} %copy.19.count_hbm, f32[3,16384]{1,0:T(4,128)S(1)} %copy-done.1, ...), custom_call_target="tpu_custom_call" | custom-call | tf_op jit(solution)/shard_map/primal_dual_adjoint/pallas_call | solution.py:407
  85.8 0.5 slice_bitcast_fusion
  86.3 0.6 copy.20
  87.0 0.6 copy.21
Async XLA Ops:
  1.3 2.2 %copy-start = (bf16[1,1,32,256,256]{4,3,2,1,0:T(8,128)(2,1)S(1)}, bf16[1,1,32,256,256]{4,3,2,1,0:T(8,128)(2,1)}, u32[]{:S(2)}) copy-start(bf16[1,1,32,256,256]{4,3,2,1,0:T(8,128)(2,1)} %param.14) | copy-start | bytes 12582916
  3.5 0.9 %copy-start.1 = (f32[3,16384]{1,0:T(4,128)S(1)}, f32[3,16384]{1,0:T(4,128)}, u32[]{:S(2)}) copy-start(f32[3,16384]{1,0:T(4,128)} %primal_hbm.1) | copy-start | bytes 589828
  4.4 0.9 %copy-start.2 = (f32[3,16384]{1,0:T(4,128)S(1)}, f32[3,16384]{1,0:T(4,128)}, u32[]{:S(2)}) copy-start(f32[3,16384]{1,0:T(4,128)} %dual_hbm.1) | copy-start | bytes 589828
  5.4 0.9 %copy-start.3 = (s32[3,16384]{1,0:T(4,128)S(1)}, s32[3,16384]{1,0:T(4,128)}, u32[]{:S(2)}) copy-start(s32[3,16384]{1,0:T(4,128)} %pmask_hbm.1) | copy-start | bytes 589828
  6.3 0.9 %copy-start.4 = (s32[3,16384]{1,0:T(4,128)S(1)}, s32[3,16384]{1,0:T(4,128)}, u32[]{:S(2)}) copy-start(s32[3,16384]{1,0:T(4,128)} %dmask_hbm.1) | copy-start | bytes 589828
  7.3 0.8 copy-start.5
  8.1 0.8 copy-start.6
  9.0 0.8 copy-start.7
  9.8 0.8 copy-start.8
  10.6 0.8 copy-start.9
  11.5 0.7 copy-start.10
  12.1 0.7 copy-start.11
  12.8 0.7 copy-start.12

commit v2 on v1

--- a/solution.py
+++ b/solution.py
@@ -138,7 +138,7 @@
     iota = lax.broadcasted_iota(jnp.int32, (blocks, LANES), 0)
 
     def spread(s, index_ref, halves):
-        keep = iota == index_ref[0, s] + blocks * jnp.maximum(s + 1 - count_s[0, 0], 0)
+        keep = iota == index_ref[0, s] + blocks * jnp.maximum(s + 1 - count_s[0], 0)
         return [
             jnp.where(keep, jnp.broadcast_to(h, (blocks, LANES)), 0.0).astype(BF16) for h in halves
         ]
@@ -402,7 +402,7 @@
     c_shape = (n_col, rows // n_col // LANES, LANES)
     zq, cq = z_shape[1], c_shape[1]
     blocks = rows // width
-    any_spec = pl.BlockSpec(memory_space=pl.ANY)
+    any_spec = pl.BlockSpec(memory_space=pltpu.HBM)
     phases = 4 * iters + 5
     outs = pl.pallas_call(
         functools.partial(kernel, (n_row, n_col, iters, slots)),
@@ -417,7 +417,7 @@
             pltpu.VMEM((slots, width, width), BF16),
             pltpu.SMEM((1, slots), jnp.int32),
             pltpu.SMEM((1, slots), jnp.int32),
-            pltpu.SMEM((1, 1), jnp.int32),
+            pltpu.SMEM((1,), jnp.int32),
             pltpu.SMEM((1, 2), F32),
             pltpu.VMEM((iters, columns // n_row), F32),
             pltpu.VMEM((iters, rows), F32),
@@ -456,14 +456,14 @@
             pltpu.SemaphoreType.DMA((phases,)),
         ],
         compiler_params=pltpu.CompilerParams(
-            collective_id=0, has_side_effects=True, vmem_limit_bytes=40 << 20
+            collective_id=0, has_side_effects=True, vmem_limit_bytes=64 << 20
         ),
         name="primal_dual_adjoint",
     )(
         tile_data.reshape(slots, width, width),
         tile_row_block.reshape(1, slots),
         tile_column_block.reshape(1, slots),
-        tile_count.reshape(1, 1),
+        tile_count.reshape(1),
         saved_primal,
         saved_dual,
         primal_mask,

time: 88.1 us -> 77.7 us (0.88)
  local copies, waits for them, and re-layouts: 13.9 us -> 3.82 us
    unnamed x28 -> x2, local copies, waits for them, and re-layouts: 13.4 us -> 2.72 us
where the time goes in v2:
time: 77.7 us; the launch traced here: 77.6 us
  Pallas kernels  72.4 us (93%)
  local copies, waits for them, and re-layouts  3.82 us (5%)
  between operations  1.29 us (2%)
    pallas_call x1, Pallas kernels, local(): pl.pallas_call(functools.partial(kernel, (n_row, n_col, iters, slots)), o...  72.4 us
    unnamed x2, local copies, waits for them, and re-layouts  2.72 us

profile of v2, /device:TPU:1, one launch (start us, length us, event | category | flops | bytes accessed | tf_op | source)
XLA Modules:
  0.0 77.6 jit_solution(6513499112604732636)
XLA Ops:
  1.3 72.4 %primal_dual_adjoint.1 = (f32[8,16,128]{2,1,0:T(8,128)}, f32[4,128]{1,0:T(4,128)}, f32[1,128]{1,0:T(1,128)}) custom-call(bf16[32,256,256]{2,1,0:T(8,128)(2,1)} %bitcast.15, s32[1,32]{1,0:T(1,128)} %bitcast.23, s32[1,32]{1,0:T(1,128)} %bitcast.24, s32[1]{0:T(128)} %bitcast.14.count_hbm, f32[3,16384]{1,0:T(4,128)} %primal_hbm.1, f32[3,16384]{1,0:T(4,128)} %dual_hbm.1, ...), custom_call_target="tpu_custom_call" | custom-call | tf_op jit(solution)/shard_map/primal_dual_adjoint/pallas_call | solution.py:407
  73.7 1.1 %slice_bitcast_fusion = f32[2]{0:T(128)} fusion(f32[1,128]{1,0:T(1,128)} %get-tuple-element.8), kind=kLoop, calls=%fused_computation | loop fusion | bytes 16 | tf_op jit(solution)/shard_map/squeeze | solution.py:478
  74.8 1.5 %copy.20 = f32[16384]{0:T(1024)} copy(f32[16384]{0:T(1024)} %bitcast.21) | data formatting | bytes 131072
  76.3 1.2 %copy.21 = f32[512]{0:T(512)} copy(f32[512]{0:T(512)} %bitcast.22) | data formatting | bytes 4096

commit v3 on v2

v3 whole, which is shorter than its diff:
```python
import functools
import math

import jax
import jax.numpy as jnp
from jax import lax
from jax.experimental import pallas as pl
from jax.experimental.pallas import tpu as pltpu
from jax.sharding import PartitionSpec as P

F32 = jnp.float32
BF16 = jnp.bfloat16
LANES = 128
NN = (((1,), (0,)), ((), ()))
NT = (((1,), (1,)), ((), ()))


def ring_offsets(n):
    return sorted(range(1, n), key=lambda r: -min(r, n - r))


def kernel(
    dims,
    tiles_hbm,
    rb_hbm,
    cb_hbm,
    count_hbm,
    primal_hbm,
    dual_hbm,
    pmask_hbm,
    dmask_hbm,
    cost_hbm,
    demand_hbm,
    upper_hbm,
    steps_hbm,
    pcot_hbm,
    dcot_hbm,
    padj_hbm,
    dadj_hbm,
    grad_hbm,
    tiles,
    turned,
    rb_s,
    cb_s,
    count_s,
    steps_s,
    primal_in,
    dual_in,
    pmask_in,
    dmask_in,
    cost,
    demand,
    upper,
    pcot,
    dcot,
    primal,
    pmask,
    dmask,
    lhs,
    picked,
    picked_mask,
    p_rows,
    z_lin,
    z_send,
    z_recv,
    z3_send,
    z3_recv,
    hilo,
    prod_all,
    ax_all,
    x_all,
    rm_all,
    idx_all,
    c_lin,
    c_send,
    c_recv,
    d_all,
    out_all,
    dadj,
    sz_all,
    sc_all,
    grad,
    in_sem,
    send_sem,
    recv_sem,
):
    n_row, n_col, iters, slots = dims
    me_r = lax.axis_index("row")
    me_c = lax.axis_index("col")
    blocks = 64
    width = tiles.shape[-1]
    group = 8

    def fetch(i, src, dst):
        copy = pltpu.make_async_copy(src, dst, in_sem.at[i])
        copy.start()
        return copy

    z_lanes = primal_in.shape[1]
    small = [
        fetch(0, rb_hbm, rb_s),
        fetch(1, cb_hbm, cb_s),
        fetch(2, count_hbm, count_s),
        fetch(3, steps_hbm, steps_s),
        fetch(4, dmask_hbm, dmask_in),
        fetch(5, dcot_hbm, dcot),
    ]
    tile_copies = [
        fetch(14 + g, tiles_hbm.at[pl.ds(g * group, group)], tiles.at[pl.ds(g * group, group)])
        for g in range(slots // group)
    ]
    z_at = pl.ds(pl.multiple_of(me_r * z_lanes, LANES), z_lanes)
    rest = [
        fetch(6, dual_hbm, dual_in),
        fetch(7, primal_hbm.at[:, z_at], primal_in),
        fetch(8, pmask_hbm, pmask_in),
        fetch(9, cost_hbm.at[me_r], cost),
        fetch(10, upper_hbm.at[me_r], upper),
        fetch(11, pcot_hbm, pcot),
        fetch(12, demand_hbm.at[me_c], demand),
    ]

    z_peers = [(r, lax.rem(me_r + r, n_row)) for r in ring_offsets(n_row)]
    c_peers = [(r, lax.rem(me_c + r, n_col)) for r in range(1, n_col)]
    barrier = pltpu.get_barrier_semaphore()
    for _, r in z_peers:
        pl.semaphore_signal(barrier, inc=1, device_id={"row": r})
    for _, c in c_peers:
        pl.semaphore_signal(barrier, inc=1, device_id={"col": c})

    def send(sem, src, dst, peer):
        pltpu.make_async_remote_copy(
            src_ref=src,
            dst_ref=dst,
            send_sem=send_sem.at[sem],
            recv_sem=recv_sem.at[sem],
            device_id=peer,
            device_id_type=pl.DeviceIdType.MESH,
        ).start()

    def gather_z(sem, here):
        for _, peer in z_peers:
            send(sem, here, here, {"row": peer})

    def gather_c(sem, here):
        for _, peer in c_peers:
            send(sem, here, here, {"col": peer})

    def arrive(sem, ref):
        pltpu.make_async_copy(ref, ref, recv_sem.at[sem]).wait()

    def left(sem, ref):
        pltpu.make_async_copy(ref, ref, send_sem.at[sem]).wait()

    def others(n):
        return pl.ds(0, n - 1)

    SCATTER, PROD, FOLD, DUAL, AX = range(5)

    def phase(k, which):
        return 5 * k + which

    Z3, XG, RM, OUT, SZ, SC, IDX = (5 * iters + i for i in range(7))

    for copy in small:
        copy.wait()
    tau = steps_s[0, 0]
    sigma = steps_s[0, 1]
    weights = [(k + 1.0) / (k + 2.0) for k in range(iters)]
    last = iters - 1

    iota = lax.broadcasted_iota(jnp.int32, (blocks, LANES), 0)
    iota8 = lax.broadcasted_iota(jnp.int32, (group, width), 0)

    def live_block(s, index_ref):
        return index_ref[0, s] + blocks * jnp.maximum(s + 1 - count_s[0], 0)

    def spread(s, index_ref, halves):
        keep = iota == live_block(s, index_ref)
        return [
            jnp.where(keep, jnp.broadcast_to(h, (blocks, LANES)), 0.0).astype(BF16) for h in halves
        ]

    def dot(a, b):
        return lax.dot_general(a, b, NN, preferred_element_type=F32)

    def slot_products(value, wait=None):
        hi = value.astype(BF16).astype(F32)
        lo = value - hi
        his, los = [], []
        for g in range(slots // group):
            if wait is not None:
                wait[g].wait()
            cut = slice(g * group, (g + 1) * group)
            rows = jnp.concatenate([hi[cut], lo[cut]], axis=0).astype(BF16)
            ph = jnp.zeros((group, width), F32)
            po = jnp.zeros((group, width), F32)
            for i in range(group):
                both = dot(rows, tiles[g * group + i])
                ph = jnp.where(iota8 == i, both[:group], ph)
                po = jnp.where(iota8 == i, both[group:], po)
            his.append(ph)
            los.append(po)
        return jnp.concatenate(his, axis=0), jnp.concatenate(los, axis=0)

    def scatter(hot, value):
        a = value.astype(BF16)
        r = value - a.astype(F32)
        b = r.astype(BF16)
        c = (r - b.astype(F32)).astype(BF16)
        return dot(hot, jnp.concatenate([a, b, c, jnp.zeros_like(a)], axis=0))

    def apply_duals():
        for s in range(slots):
            r = rb_s[0, s]
            for v in range(iters):
                halves = [dual_in[pl.ds(v, 1), pl.ds((2 * r + h) * LANES, LANES)] for h in range(2)]
                for h, value in enumerate(spread(s, cb_s, halves)):
                    lhs[
                        v * blocks : (v + 1) * blocks,
                        s * width + h * LANES : s * width + (h + 1) * LANES,
                    ] = value
        return dot(lhs[...], tiles[...].reshape(slots * width, width))

    def apply_forward():
        acc = jnp.zeros((blocks, width), F32)
        for s in range(slots):
            c = cb_s[0, s]
            b = lax.div(c, 8)
            i = 2 * lax.rem(c, 8)
            halves = [p_rows[b, pl.ds(i, 1), :], p_rows[b, pl.ds(i + 1, 1), :]]
            row = jnp.concatenate(spread(s, rb_s, halves), axis=1)
            acc = acc + dot(row, turned[s])
        return acc

    def store_z(dst, value):
        for j in range(n_row):
            for h in range(2):
                dst[j, pl.ds(h, 8, stride=2), :] = value[
                    8 * j : 8 * j + 8, h * LANES : (h + 1) * LANES
                ]

    for s in range(slots):
        r = rb_s[0, s]
        a = lax.div(r, 2)
        b = 2 * lax.rem(r, 2)
        for h in range(2):
            cut = slice(h * LANES, (h + 1) * LANES)
            picked[s : s + 1, cut] = dcot[a, pl.ds(b + h, 1), :]
            picked_mask[s : s + 1, cut] = dmask_in[pl.ds(last, 1), pl.ds((2 * r + h) * LANES, LANES)]
    start = picked_mask[...].astype(F32) * weights[last] * picked[...]

    tau_local = jnp.zeros((), F32)
    sigma_local = jnp.zeros((), F32)
    anchor_x = anchor_y = None
    ax = ay = d = None
    hot = hot_all = None

    for k in reversed(range(iters)):
        weight = weights[k]
        if k == last:
            ph, po = slot_products(start, tile_copies)
        else:
            for s in range(slots):
                r = rb_s[0, s]
                a = lax.div(r, 2)
                b = 2 * lax.rem(r, 2)
                for h in range(2):
                    cut = slice(h * LANES, (h + 1) * LANES)
                    picked[s : s + 1, cut] = d_all[k, a, pl.ds(b + h, 1), :]
            ph, po = slot_products(picked[...])
        prod_all[k, me_r] = ph.astype(BF16)
        if k == last:
            lane2 = lax.broadcasted_iota(jnp.int32, (1, 2 * LANES), 1)
            lane = lax.broadcasted_iota(jnp.int32, (1, LANES), 1)
            mine = jnp.full((1, 2 * LANES), -1, jnp.int32)
            own = jnp.full((1, LANES), -1, jnp.int32)
            for s in range(slots):
                block = live_block(s, cb_s)
                mine = jnp.where(lane2 == me_r * slots + s, block, mine)
                own = jnp.where(lax.rem(lane, slots) == s, block, own)
            idx_all[me_r] = mine.astype(F32)
            hot = jnp.where(iota == own, 1.0, 0.0).astype(BF16)
            pl.semaphore_wait(barrier, len(z_peers) + len(c_peers))
        gather_z(phase(k, PROD), prod_all.at[k, me_r])
        if k == last:
            gather_z(IDX, idx_all.at[me_r])
        store_z(z_send.at[k], scatter(hot, ph))
        for r, peer in z_peers:
            send(phase(k, SCATTER), z_send.at[k, peer], z_recv.at[k, r - 1], {"row": peer})
        store_z(hilo.at[k], scatter(hot, ph + po))
        if k == last:
            for copy in rest:
                copy.wait()
            duals = apply_duals()
            for i in range(iters):
                for j in range(n_row):
                    for h in range(2):
                        z3_send[j, i, pl.ds(h, 8, stride=2), :] = duals[
                            i * blocks + 8 * j : i * blocks + 8 * j + 8,
                            h * LANES : (h + 1) * LANES,
                        ]
            for i in range(iters):
                for j in range(n_row):
                    for q in range(16):
                        at = (16 * j + q) * LANES
                        pmask[i, j, q : q + 1, :] = pmask_in[i : i + 1, at : at + LANES]
                for q in range(16):
                    primal[i, q : q + 1, :] = primal_in[i : i + 1, q * LANES : (q + 1) * LANES]
                for q in range(4):
                    at = pl.multiple_of(me_c * (4 * LANES) + q * LANES, LANES)
                    dmask[i, q : q + 1, :] = dmask_in[i : i + 1, pl.ds(at, LANES)].astype(F32)
            for s in range(slots):
                turned[s] = tiles[s].T
            ax = pcot[me_r]
            ay = dcot[me_c]
            anchor_x = (1.0 - weight) * ax
            anchor_y = (1.0 - weight) * ay
            d = dmask[k] * weight * ay
        else:
            if k == last - 1:
                arrive(XG, x_all.at[others(n_row)])
                arrive(RM, rm_all.at[others(n_row)])
                sigma_local = sigma_local - jnp.sum(hilo[last] * x_all[:, last].astype(F32))
            sigma_local = sigma_local - jnp.sum(hilo[k] * x_all[:, k].astype(F32))
        sigma_local = sigma_local + jnp.sum(d * demand[...])
        if k == 0:
            held = pmask[0, me_r].astype(F32) * weight * ax * primal[0]
            tau_local = tau_local - jnp.sum(held) + (2.0 * sigma) * jnp.sum(z_send[0] * rm_all[...])
            lane = lax.broadcasted_iota(jnp.int32, (1, LANES), 1)
            sz_all[me_r] = jnp.where(lane == 0, tau_local, jnp.where(lane == 1, sigma_local, 0.0))
            gather_z(SZ, sz_all.at[me_r])
        if k == last:
            arrive(IDX, idx_all.at[others(n_row)])
            index = idx_all[0]
            for r in range(1, n_row):
                index = jnp.maximum(index, idx_all[r])
            rows = lax.broadcasted_iota(jnp.int32, (blocks, 2 * LANES), 0).astype(F32)
            hot_all = jnp.where(rows == index, 1.0, 0.0).astype(BF16)
            ax_full = pcot[...]
        else:
            arrive(phase(k + 1, AX), ax_all.at[k, others(n_row)])
            ax_full = ax_all[k]
        arrive(phase(k, PROD), prod_all.at[k, others(n_row)])
        store_z(z_lin, dot(hot_all, prod_all[k].reshape(n_row * slots, width)))
        p_full = pmask[k].astype(F32) * (weight * ax_full - (2.0 * sigma) * z_lin[...])
        p_rows[...] = p_full.astype(BF16).astype(F32)
        if k == last:
            for r, peer in z_peers:
                send(Z3, z3_send.at[peer], z3_recv.at[r - 1], {"row": peer})
        image = apply_forward()
        c_lin[pl.ds(0, blocks, stride=2), :] = image[:, :LANES]
        c_lin[pl.ds(1, blocks, stride=2), :] = image[:, LANES:]
        c_send[k] = c_lin[...].reshape(n_col, 4, LANES)
        for r, peer in c_peers:
            send(phase(k, FOLD), c_send.at[k, peer], c_recv.at[k, r - 1], {"col": peer})
        if k == 0:
            arrive(SZ, sz_all.at[others(n_row)])
            total = sz_all[0]
            for r in range(1, n_row):
                total = total + sz_all[r]
            sc_all[me_c] = total
            gather_c(SC, sc_all.at[me_c])
        arrive(phase(k, SCATTER), z_recv.at[k])
        back = z_send[k, me_r]
        for r in range(n_row - 1):
            back = back + z_recv[k, r]
        if k != last:
            anchor_x = anchor_x + (1.0 - weight) * ax
        p = pmask[k, me_r].astype(F32) * (weight * ax - (2.0 * sigma) * back)
        ax = p + sigma * back
        if k > 0:
            ax_all[k - 1, me_r] = ax
            gather_z(phase(k, AX), ax_all.at[k - 1, me_r])
        else:
            out_all[me_r] = ax + anchor_x
            gather_z(OUT, out_all.at[me_r])
        if k == last:
            p_last = p
        elif k > 0:
            tau_local = tau_local - jnp.sum(p * primal[k])
        arrive(phase(k, FOLD), c_recv.at[k])
        rows = c_send[k, me_c]
        for r in range(n_col - 1):
            rows = rows + c_recv[k, r]
        ay = d + tau * rows
        if k > 0:
            weight = weights[k - 1]
            anchor_y = anchor_y + (1.0 - weight) * ay
            d = dmask[k - 1] * weight * ay
            d_all[k - 1, me_c] = d
            gather_c(phase(k - 1, DUAL), d_all.at[k - 1, me_c])
            if k == last:
                arrive(Z3, z3_recv)
                for i in range(iters):
                    column = z3_send[me_r, i]
                    for r in range(n_row - 1):
                        column = column + z3_recv[r, i]
                    reduced = cost[...] - column
                    saved = primal[i]
                    half = jnp.minimum(jnp.maximum(saved - tau * reduced, 0.0), upper[...])
                    x_all[me_r, i] = (2.0 * half - saved).astype(BF16)
                    primal[i] = reduced
                rm_all[me_r] = pmask[0, me_r].astype(F32) * primal[0]
                gather_z(XG, x_all.at[me_r])
                gather_z(RM, rm_all.at[me_r])
                tau_local = tau_local - jnp.sum(p_last * primal[last])
            arrive(phase(k - 1, DUAL), d_all.at[k - 1, others(n_col)])

    dadj[...] = ay + anchor_y
    dadj_copy = pltpu.make_async_copy(dadj, dadj_hbm, in_sem.at[1])
    dadj_copy.start()
    arrive(OUT, out_all.at[others(n_row)])
    padj_copy = pltpu.make_async_copy(out_all, padj_hbm, in_sem.at[0])
    padj_copy.start()
    arrive(SC, sc_all.at[others(n_col)])
    total = sc_all[0]
    for c in range(1, n_col):
        total = total + sc_all[c]
    lane = lax.broadcasted_iota(jnp.int32, (1, LANES), 1)
    columns = float(n_col * blocks * width)
    lines = float(n_row * blocks * width)
    scaled = total * jnp.where(lane == 0, 1.0 / math.sqrt(columns), 1.0 / math.sqrt(lines))
    grad[...] = scaled[:, :2]
    grad_copy = pltpu.make_async_copy(grad, grad_hbm, in_sem.at[2])
    grad_copy.start()

    for k in range(iters):
        left(phase(k, SCATTER), z_recv.at[k])
        left(phase(k, PROD), prod_all.at[k, others(n_row)])
        left(phase(k, FOLD), c_recv.at[k])
        if k < last:
            left(phase(k, DUAL), d_all.at[k, others(n_col)])
        if k > 0:
            left(phase(k, AX), ax_all.at[k - 1, others(n_row)])
    left(Z3, z3_recv)
    left(XG, x_all.at[others(n_row)])
    left(RM, rm_all.at[others(n_row)])
    left(IDX, idx_all.at[others(n_row)])
    left(OUT, out_all.at[others(n_row)])
    left(SZ, sz_all.at[others(n_row)])
    left(SC, sc_all.at[others(n_col)])
    padj_copy.wait()
    dadj_copy.wait()
    grad_copy.wait()


def hand_over(padj_in, dadj_in, grad_in, padj, dadj, grad, sem):
    copies = [
        pltpu.make_async_copy(src, dst, sem.at[i])
        for i, (src, dst) in enumerate(((padj_in, padj), (dadj_in, dadj), (grad_in, grad)))
    ]
    for copy in copies:
        copy.start()
    for copy in copies:
        copy.wait()


def local(
    tile_data,
    tile_row_block,
    tile_column_block,
    tile_count,
    saved_primal,
    saved_dual,
    primal_mask,
    dual_mask,
    cost_vector,
    demand,
    upper_bound,
    step_sizes,
    primal_cotangent,
    dual_cotangent,
):
    n_row = lax.axis_size("row")
    n_col = lax.axis_size("col")
    slots, width = tile_data.shape[2], tile_data.shape[-1]
    iters = saved_primal.shape[0]
    rows = saved_dual.shape[1]
    columns = saved_primal.shape[1]
    z_shape = (n_row, columns // n_row // LANES, LANES)
    c_shape = (n_col, rows // n_col // LANES, LANES)
    zq, cq = z_shape[1], c_shape[1]
    blocks = rows // width
    any_spec = pl.BlockSpec(memory_space=pltpu.HBM)
    phases = 5 * iters + 7
    outs = pl.pallas_call(
        functools.partial(kernel, (n_row, n_col, iters, slots)),
        out_shape=(
            jax.ShapeDtypeStruct(z_shape, F32),
            jax.ShapeDtypeStruct(c_shape[1:], F32),
            jax.ShapeDtypeStruct((1, 2), F32),
        ),
        in_specs=[any_spec] * 14,
        out_specs=(any_spec,) * 3,
        scratch_shapes=[
            pltpu.VMEM((slots, width, width), BF16),
            pltpu.VMEM((slots, width, width), BF16),
            pltpu.SMEM((1, slots), jnp.int32),
            pltpu.SMEM((1, slots), jnp.int32),
            pltpu.SMEM((1,), jnp.int32),
            pltpu.SMEM((1, 2), F32),
            pltpu.VMEM((iters, columns // n_row), F32),
            pltpu.VMEM((iters, rows), F32),
            pltpu.VMEM((iters, columns), jnp.int32),
            pltpu.VMEM((iters, rows), jnp.int32),
            pltpu.VMEM(z_shape[1:], F32),
            pltpu.VMEM(c_shape[1:], F32),
            pltpu.VMEM(z_shape[1:], F32),
            pltpu.VMEM(z_shape, F32),
            pltpu.VMEM(c_shape, F32),
            pltpu.VMEM((iters, zq, LANES), F32),
            pltpu.VMEM((iters,) + z_shape, jnp.int32),
            pltpu.VMEM((iters, cq, LANES), F32),
            pltpu.VMEM((iters * blocks, slots * width), BF16),
            pltpu.VMEM((slots, width), F32),
            pltpu.VMEM((slots, width), jnp.int32),
            pltpu.VMEM(z_shape, F32),
            pltpu.VMEM(z_shape, F32),
            pltpu.VMEM((iters,) + z_shape, F32),
            pltpu.VMEM((iters, n_row - 1, zq, LANES), F32),
            pltpu.VMEM((n_row, iters, zq, LANES), F32),
            pltpu.VMEM((n_row - 1, iters, zq, LANES), F32),
            pltpu.VMEM((iters,) + z_shape, F32),
            pltpu.VMEM((iters, n_row, slots, width), BF16),
            pltpu.VMEM((iters - 1,) + z_shape, F32),
            pltpu.VMEM((n_row, iters, zq, LANES), BF16),
            pltpu.VMEM(z_shape, F32),
            pltpu.VMEM((n_row, 1, 2 * LANES), F32),
            pltpu.VMEM((rows // LANES, LANES), F32),
            pltpu.VMEM((iters,) + c_shape, F32),
            pltpu.VMEM((iters, n_col - 1, cq, LANES), F32),
            pltpu.VMEM((iters - 1,) + c_shape, F32),
            pltpu.VMEM(z_shape, F32),
            pltpu.VMEM(c_shape[1:], F32),
            pltpu.VMEM((n_row, 1, LANES), F32),
            pltpu.VMEM((n_col, 1, LANES), F32),
            pltpu.VMEM((1, 2), F32),
            pltpu.SemaphoreType.DMA((14 + slots // 8,)),
            pltpu.SemaphoreType.DMA((phases,)),
            pltpu.SemaphoreType.DMA((phases,)),
        ],
        compiler_params=pltpu.CompilerParams(
            collective_id=0, has_side_effects=True, vmem_limit_bytes=64 << 20
        ),
        name="primal_dual_adjoint",
    )(
        tile_data.reshape(slots, width, width),
        tile_row_block.reshape(1, slots),
        tile_column_block.reshape(1, slots),
        tile_count.reshape(1),
        saved_primal,
        saved_dual,
        primal_mask,
        dual_mask,
        cost_vector.reshape(z_shape),
        demand.reshape(c_shape),
        upper_bound.reshape(z_shape),
        step_sizes.reshape(1, 2),
        primal_cotangent.reshape(z_shape),
        dual_cotangent.reshape(c_shape),
    )
    padj, dadj, grad = pl.pallas_call(
        hand_over,
        out_shape=tuple(jax.ShapeDtypeStruct(out.shape, F32) for out in outs),
        in_specs=[any_spec] * 3,
        out_specs=(any_spec,) * 3,
        scratch_shapes=[pltpu.SemaphoreType.DMA((3,))],
        compiler_params=pltpu.CompilerParams(vmem_limit_bytes=64 << 20),
        name="hand_over",
    )(*outs)
    return (padj.reshape(columns), dadj.reshape(rows // n_col), grad.reshape(2))


def solution(mesh):
    placed = (
        P("row", "col", None, None, None),
        P("row", "col", None),
        P("row", "col", None),
        P("row", "col"),
        P(None, "col"),
        P(None, "row"),
        P(None, "col"),
        P(None, "row"),
        P("col"),
        P("row"),
        P("col"),
        P(),
        P("col"),
        P("row"),
    )
    return jax.shard_map(
        local,
        mesh=mesh,
        in_specs=placed,
        out_specs=(P("col"), P(("row", "col")), P()),
        check_vma=False,
    )
```

time: 77.7 us -> 66.9 us (0.86)
  Pallas kernels: 72.4 us -> 65.5 us
  local copies, waits for them, and re-layouts: 3.82 us -> 0 us
    pallas_call x1, Pallas kernels: 72.4 us -> 62.3 us  [local(): pl.pallas_call(functools.partial(kernel, (n_row, n_col, iters, slots)), o...]
    pallas_call x0 -> x1, Pallas kernels: none -> 3.19 us  [local(): pl.pallas_call(hand_over, out_shape=tuple((jax.ShapeDtypeStruct(out.shape...]
    unnamed x2 -> x0, local copies, waits for them, and re-layouts: 2.72 us -> none
    squeeze x1 -> x0, local copies, waits for them, and re-layouts: 1.11 us -> none  [local(): outs[2][0, :2]]
where the time goes in v3:
time: 66.9 us; the launch traced here: 66.8 us
  Pallas kernels  65.5 us (98%)
  between operations  1.29 us (2%)
    pallas_call x1, Pallas kernels, local(): pl.pallas_call(functools.partial(kernel, (n_row, n_col, iters, slots)), o...  62.3 us
    pallas_call x1, Pallas kernels, local(): pl.pallas_call(hand_over, out_shape=tuple((jax.ShapeDtypeStruct(out.shape...  3.19 us

profile of v3, /device:TPU:1, one launch (start us, length us, event | category | flops | bytes accessed | tf_op | source)
XLA Modules:
  0.0 66.8 jit_solution(6186704810379926021)
XLA Ops:
  1.3 62.3 %primal_dual_adjoint.1 = (f32[8,16,128]{2,1,0:T(8,128)}, f32[4,128]{1,0:T(4,128)}, f32[1,2]{1,0:T(1,128)}) custom-call(bf16[32,256,256]{2,1,0:T(8,128)(2,1)} %bitcast.14, s32[1,32]{1,0:T(1,128)} %bitcast.20, s32[1,32]{1,0:T(1,128)} %bitcast.21, s32[1]{0:T(128)} %bitcast.13.count_hbm, f32[3,16384]{1,0:T(4,128)} %primal_hbm.1, f32[3,16384]{1,0:T(4,128)} %dual_hbm.1, ...), custom_call_target="tpu_custom_call" | custom-call | tf_op jit(solution)/shard_map/primal_dual_adjoint/pallas_call | solution.py:487
  63.6 3.2 %hand_over.1 = (f32[8,16,128]{2,1,0:T(8,128)}, f32[4,128]{1,0:T(4,128)}, f32[1,2]{1,0:T(1,128)}) custom-call(f32[8,16,128]{2,1,0:T(8,128)} %get-tuple-element.9.padj_in, f32[4,128]{1,0:T(4,128)} %get-tuple-element.10.dadj_in, f32[1,2]{1,0:T(1,128)} %get-tuple-element.11.grad_in), custom_call_target="tpu_custom_call" | custom-call | tf_op jit(solution)/shard_map/hand_over/pallas_call | solution.py:563

commit v4 on v3

--- a/solution.py
+++ b/solution.py
@@ -121,7 +121,17 @@
     ]
 
     z_peers = [(r, lax.rem(me_r + r, n_row)) for r in ring_offsets(n_row)]
-    c_peers = [(r, lax.rem(me_c + r, n_col)) for r in range(1, n_col)]
+    side = math.isqrt(n_col // 2)
+    x, y, core = lax.div(me_c, 2 * side), lax.rem(lax.div(me_c, 2), side), lax.rem(me_c, 2)
+    steps = [(dx, dy, dz) for dx in range(side) for dy in range(side) for dz in range(2)][1:]
+    steps.sort(key=lambda t: -min(t[0], side - t[0]) - min(t[1], side - t[1]) - 0.5 * t[2])
+    c_peers = [
+        (
+            i + 1,
+            (lax.rem(x + dx, side) * side + lax.rem(y + dy, side)) * 2 + lax.rem(core + dz, 2),
+        )
+        for i, (dx, dy, dz) in enumerate(steps)
+    ]
     barrier = pltpu.get_barrier_semaphore()
     for _, r in z_peers:
         pl.semaphore_signal(barrier, inc=1, device_id={"row": r})
@@ -239,6 +249,10 @@
                 dst[j, pl.ds(h, 8, stride=2), :] = value[
                     8 * j : 8 * j + 8, h * LANES : (h + 1) * LANES
                 ]
+
+    def send_exact(k):
+        for r, peer in z_peers:
+            send(phase(k, SCATTER), z_send.at[k, peer], z_recv.at[k, r - 1], {"row": peer})
 
     for s in range(slots):
         r = rb_s[0, s]
@@ -286,8 +300,8 @@
         if k == last:
             gather_z(IDX, idx_all.at[me_r])
         store_z(z_send.at[k], scatter(hot, ph))
-        for r, peer in z_peers:
-            send(phase(k, SCATTER), z_send.at[k, peer], z_recv.at[k, r - 1], {"row": peer})
+        if k == 0:
+            send_exact(k)
         store_z(hilo.at[k], scatter(hot, ph + po))
         if k == last:
             for copy in rest:
@@ -342,6 +356,8 @@
             arrive(phase(k + 1, AX), ax_all.at[k, others(n_row)])
             ax_full = ax_all[k]
         arrive(phase(k, PROD), prod_all.at[k, others(n_row)])
+        if k > 0:
+            send_exact(k)
         store_z(z_lin, dot(hot_all, prod_all[k].reshape(n_row * slots, width)))
         p_full = pmask[k].astype(F32) * (weight * ax_full - (2.0 * sigma) * z_lin[...])
         p_rows[...] = p_full.astype(BF16).astype(F32)
@@ -445,15 +461,22 @@
     grad_copy.wait()
 
 
-def hand_over(padj_in, dadj_in, grad_in, padj, dadj, grad, sem):
+def hand_over(padj_in, dadj_in, grad_in, padj, dadj, grad, padj_v, dadj_v, grad_v, sem):
     copies = [
         pltpu.make_async_copy(src, dst, sem.at[i])
-        for i, (src, dst) in enumerate(((padj_in, padj), (dadj_in, dadj), (grad_in, grad)))
+        for i, (src, dst) in enumerate(((padj_in, padj_v), (dadj_in, dadj_v), (grad_in, grad_v)))
     ]
     for copy in copies:
         copy.start()
-    for copy in copies:
+    outs = [
+        pltpu.make_async_copy(src, dst, sem.at[3 + i])
+        for i, (src, dst) in enumerate(((padj_v, padj), (dadj_v, dadj), (grad_v, grad)))
+    ]
+    for copy, out in zip(copies, outs):
         copy.wait()
+        out.start()
+    for out in outs:
+        out.wait()
 
 
 def local(
@@ -565,7 +588,7 @@
         out_shape=tuple(jax.ShapeDtypeStruct(out.shape, F32) for out in outs),
         in_specs=[any_spec] * 3,
         out_specs=(any_spec,) * 3,
-        scratch_shapes=[pltpu.SemaphoreType.DMA((3,))],
+        scratch_shapes=[pltpu.VMEM(out.shape, F32) for out in outs] + [pltpu.SemaphoreType.DMA((6,))],
         compiler_params=pltpu.CompilerParams(vmem_limit_bytes=64 << 20),
         name="hand_over",
     )(*outs)

time: 66.9 us -> 63 us (0.942)
  Pallas kernels: 65.5 us -> 61.5 us
    pallas_call x1, Pallas kernels: 62.3 us -> 60 us  [local(): pl.pallas_call(functools.partial(kernel, (n_row, n_col, iters, slots)), o...]
    pallas_call x1, Pallas kernels: 3.19 us -> 1.53 us  [local(): pl.pallas_call(hand_over, out_shape=tuple((jax.ShapeDtypeStruct(out.shape...]
where the time goes in v4:
time: 63 us; the launch traced here: 62.8 us
  Pallas kernels  61.5 us (98%)
  between operations  1.29 us (2%)
    pallas_call x1, Pallas kernels, local(): pl.pallas_call(functools.partial(kernel, (n_row, n_col, iters, slots)), o...  60 us
    pallas_call x1, Pallas kernels, local(): pl.pallas_call(hand_over, out_shape=tuple((jax.ShapeDtypeStruct(out.shape...  1.53 us

profile of v4, /device:TPU:1, one launch (start us, length us, event | category | flops | bytes accessed | tf_op | source)
XLA Modules:
  0.0 62.8 jit_solution(13798039044594898503)
XLA Ops:
  1.3 60.0 %primal_dual_adjoint.1 = (f32[8,16,128]{2,1,0:T(8,128)}, f32[4,128]{1,0:T(4,128)}, f32[1,2]{1,0:T(1,128)}) custom-call(bf16[32,256,256]{2,1,0:T(8,128)(2,1)} %bitcast.14, s32[1,32]{1,0:T(1,128)} %bitcast.20, s32[1,32]{1,0:T(1,128)} %bitcast.21, s32[1]{0:T(128)} %bitcast.13.count_hbm, f32[3,16384]{1,0:T(4,128)} %primal_hbm.1, f32[3,16384]{1,0:T(4,128)} %dual_hbm.1, ...), custom_call_target="tpu_custom_call" | custom-call | tf_op jit(solution)/shard_map/primal_dual_adjoint/pallas_call | solution.py:510
  61.3 1.5 %hand_over.1 = (f32[8,16,128]{2,1,0:T(8,128)}, f32[4,128]{1,0:T(4,128)}, f32[1,2]{1,0:T(1,128)}) custom-call(f32[8,16,128]{2,1,0:T(8,128)} %get-tuple-element.9.padj_in, f32[4,128]{1,0:T(4,128)} %get-tuple-element.10.dadj_in, f32[1,2]{1,0:T(1,128)} %get-tuple-element.11.grad_in), custom_call_target="tpu_custom_call" | custom-call | tf_op jit(solution)/shard_map/hand_over/pallas_call | solution.py:586

commit v5 on v4

--- a/solution.py
+++ b/solution.py
@@ -264,11 +264,22 @@
             picked_mask[s : s + 1, cut] = dmask_in[pl.ds(last, 1), pl.ds((2 * r + h) * LANES, LANES)]
     start = picked_mask[...].astype(F32) * weights[last] * picked[...]
 
+    lane2 = lax.broadcasted_iota(jnp.int32, (1, 2 * LANES), 1)
+    lane = lax.broadcasted_iota(jnp.int32, (1, LANES), 1)
+    mine = jnp.full((1, 2 * LANES), -1, jnp.int32)
+    own = jnp.full((1, LANES), -1, jnp.int32)
+    for s in range(slots):
+        block = live_block(s, cb_s)
+        mine = jnp.where(lane2 == me_r * slots + s, block, mine)
+        own = jnp.where(lax.rem(lane, slots) == s, block, own)
+    idx_all[me_r] = mine.astype(F32)
+    hot = jnp.where(iota == own, 1.0, 0.0).astype(BF16)
+
     tau_local = jnp.zeros((), F32)
     sigma_local = jnp.zeros((), F32)
     anchor_x = anchor_y = None
     ax = ay = d = None
-    hot = hot_all = None
+    hot_all = None
 
     for k in reversed(range(iters)):
         weight = weights[k]
@@ -285,23 +296,10 @@
             ph, po = slot_products(picked[...])
         prod_all[k, me_r] = ph.astype(BF16)
         if k == last:
-            lane2 = lax.broadcasted_iota(jnp.int32, (1, 2 * LANES), 1)
-            lane = lax.broadcasted_iota(jnp.int32, (1, LANES), 1)
-            mine = jnp.full((1, 2 * LANES), -1, jnp.int32)
-            own = jnp.full((1, LANES), -1, jnp.int32)
-            for s in range(slots):
-                block = live_block(s, cb_s)
-                mine = jnp.where(lane2 == me_r * slots + s, block, mine)
-                own = jnp.where(lax.rem(lane, slots) == s, block, own)
-            idx_all[me_r] = mine.astype(F32)
-            hot = jnp.where(iota == own, 1.0, 0.0).astype(BF16)
             pl.semaphore_wait(barrier, len(z_peers) + len(c_peers))
+            gather_z(IDX, idx_all.at[me_r])
         gather_z(phase(k, PROD), prod_all.at[k, me_r])
-        if k == last:
-            gather_z(IDX, idx_all.at[me_r])
         store_z(z_send.at[k], scatter(hot, ph))
-        if k == 0:
-            send_exact(k)
         store_z(hilo.at[k], scatter(hot, ph + po))
         if k == last:
             for copy in rest:
@@ -344,6 +342,7 @@
             lane = lax.broadcasted_iota(jnp.int32, (1, LANES), 1)
             sz_all[me_r] = jnp.where(lane == 0, tau_local, jnp.where(lane == 1, sigma_local, 0.0))
             gather_z(SZ, sz_all.at[me_r])
+            send_exact(k)
         if k == last:
             arrive(IDX, idx_all.at[others(n_row)])
             index = idx_all[0]

time: 63 us -> 62.1 us (0.986)
  Pallas kernels: 61.5 us -> 60.7 us
    pallas_call x1, Pallas kernels: 60 us -> 59.2 us  [local(): pl.pallas_call(functools.partial(kernel, (n_row, n_col, iters, slots)), o...]
where the time goes in v5:
time: 62.1 us; the launch traced here: 62 us
  Pallas kernels  60.7 us (98%)
  between operations  1.29 us (2%)
    pallas_call x1, Pallas kernels, local(): pl.pallas_call(functools.partial(kernel, (n_row, n_col, iters, slots)), o...  59.2 us
    pallas_call x1, Pallas kernels, local(): pl.pallas_call(hand_over, out_shape=tuple((jax.ShapeDtypeStruct(out.shape...  1.53 us

profile of v5, /device:TPU:1, one launch (start us, length us, event | category | flops | bytes accessed | tf_op | source)
XLA Modules:
  0.0 62.0 jit_solution(4505295533214270064)
XLA Ops:
  1.3 59.2 %primal_dual_adjoint.1 = (f32[8,16,128]{2,1,0:T(8,128)}, f32[4,128]{1,0:T(4,128)}, f32[1,2]{1,0:T(1,128)}) custom-call(bf16[32,256,256]{2,1,0:T(8,128)(2,1)} %bitcast.14, s32[1,32]{1,0:T(1,128)} %bitcast.20, s32[1,32]{1,0:T(1,128)} %bitcast.21, s32[1]{0:T(128)} %bitcast.13.count_hbm, f32[3,16384]{1,0:T(4,128)} %primal_hbm.1, f32[3,16384]{1,0:T(4,128)} %dual_hbm.1, ...), custom_call_target="tpu_custom_call" | custom-call | tf_op jit(solution)/shard_map/primal_dual_adjoint/pallas_call | solution.py:509
  60.4 1.5 %hand_over.1 = (f32[8,16,128]{2,1,0:T(8,128)}, f32[4,128]{1,0:T(4,128)}, f32[1,2]{1,0:T(1,128)}) custom-call(f32[8,16,128]{2,1,0:T(8,128)} %get-tuple-element.9.padj_in, f32[4,128]{1,0:T(4,128)} %get-tuple-element.10.dadj_in, f32[1,2]{1,0:T(1,128)} %get-tuple-element.11.grad_in), custom_call_target="tpu_custom_call" | custom-call | tf_op jit(solution)/shard_map/hand_over/pallas_call | solution.py:585
